TPU v7x, 256 devices: a whole 4x4x8 slice. The times are simulated.
256 devices in a mesh: tm: 8 (over y_hi, x), cells: 32 (over z, y_lo, core).
Axes of the slice: x: 4, y: 4 (y_hi: 2, y_lo: 2; y = y_hi * 2 + y_lo), z: 8, core: 2. Of those that a mesh axis runs over, the one named last changes fastest.
Arguments:
- footprint: float32 [8, 4, 768, 8192], P('tm', None, None, 'cells'), may hold values from -0.03125 to 0.03125
- flux: float32 [8, 8192, 2048], P('tm', 'cells'), may hold values from -6 to 6
- obs_weight: float32 [8, 768], P('tm'), may hold values from 0.2 to 5
- obs_count: int32 [8], P('tm'), may hold values from 1 to 768, 4608 in all
Outputs:
- normal_image: float32 [8, 8192, 2048], P('tm', 'cells')
Inputs may be any that keep to these rules, and one draw needn't show every extreme that they name: `obs_count`: each block has at least one valid slot; one block has all 768 slots valid.
All inputs are finite; a program needn't handle non-finite values.
Results may differ from a plain program's by a relative error of at most 0.0001.
Values sent between devices are 32-bit elements; how exact they have to be, the bound alone decides.
A program may use at most 128 MiB of HBM per device.

v0:
```python
import jax
import jax.numpy as jnp
from jax import lax
from jax.sharding import Mesh
from jax.sharding import PartitionSpec as P

CELLS = ("cells_0", "cells_1", "cells_2")


def from_behind(value, axis, by):
    devices = lax.axis_size(axis)
    pairs = [(i, i + by) for i in range(devices) if 0 <= i + by < devices]
    return lax.ppermute(value, axis, pairs)


def padded_to(lines, devices):
    spare = -lines.shape[0] % devices
    if not spare:
        return lines
    return jnp.concatenate([lines, jnp.zeros((spare, *lines.shape[1:]), lines.dtype)])


def nested_sum(value, near, far):
    lines = value.reshape(-1, *value.shape[1:][-1:])
    padded = padded_to(lines, lax.axis_size(near))
    own = lax.psum_scatter(padded, near, scatter_dimension=0, tiled=True)
    own = lax.psum(own, far)
    whole = lax.all_gather(own, near, axis=0, tiled=True)
    return whole[: len(lines)].reshape(value.shape)


def on_device(footprint, flux, obs_weight, obs_count):
    highest = lax.Precision.HIGHEST
    foot_slab = footprint[0]
    own_flux = flux[0]
    lag_count = foot_slab.shape[0]
    slot_count = foot_slab.shape[1]
    earlier = [own_flux]
    for lag_step in range(1, lag_count):
        earlier.append(from_behind(own_flux, "tm", lag_step))
    valid_rows = (jnp.arange(slot_count, dtype=jnp.int32) < obs_count[0]).astype(jnp.float32)
    row_scale = valid_rows * obs_weight[0]
    partial_value = jnp.dot(
        foot_slab[0], earlier[0], precision=highest, preferred_element_type=jnp.float32
    )
    for lag_step in range(1, lag_count):
        partial_value = partial_value + jnp.dot(
            foot_slab[lag_step],
            earlier[lag_step],
            precision=highest,
            preferred_element_type=jnp.float32,
        )
    modelled = nested_sum(partial_value, "cells_2", ("cells_0", "cells_1"))
    weighted = row_scale[:, None] * modelled
    adjoint_terms = []
    for lag_step in range(lag_count):
        adjoint_terms.append(
            lax.dot_general(
                foot_slab[lag_step],
                weighted,
                (((0,), (0,)), ((), ())),
                precision=highest,
                preferred_element_type=jnp.float32,
            )
        )
    accumulator = adjoint_terms[0]
    for lag_step in range(1, lag_count):
        accumulator = accumulator + from_behind(adjoint_terms[lag_step], "tm", -lag_step)
    return accumulator[None]


def solution(mesh):
    torus = Mesh(
        mesh.devices.reshape(mesh.shape["tm"], 8, 2, 2), ("tm", "cells_0", "cells_1", "cells_2")
    )
    placed = (P("tm", None, None, CELLS), P("tm", CELLS, None), P("tm", None), P("tm"))
    return jax.shard_map(
        on_device, mesh=torus, in_specs=placed, out_specs=P("tm", CELLS, None), check_vma=False
    )
```

profile of v0, /device:TPU:6, one launch (start us, length us, event | category | flops | bytes accessed | tf_op | source)
XLA Modules:
  0.0 543.6 jit_solution(7691611369154677838)
XLA Ops:
  6.5 0.0 reduce-scatter.2.cloned.1.call-start
  6.5 0.0 copy-start.1
  6.5 6.2 %collective-permute-start.1 = (f32[256,2048]{1,0:T(8,128)}, f32[256,2048]{1,0:T(8,128)S(1)}, u32[]{:S(2)}, u32[]{:S(2)}) collective-permute-start(f32[256,2048]{1,0:T(8,128)} %bitcast.48), channel_id=1, source_target_pairs={{0,64},{32,96},{64,128},{96,160},{128,192},{160,224},{1,65},{33,97... | collective-permute-start | bytes 6291464 | tf_op jit(solution)/shard_map/ppermute | solution.py:13
  12.7 4.0 collective-permute-start
  16.8 1.9 collective-permute-start.2
  18.7 7.0 %fusion.48 = f32[768,2048]{1,0:T(8,128)S(1)} fusion(f32[1,4,768,256]{3,2,1,0:T(8,128)} %param.4, f32[1,256,2048]{2,1,0:T(8,128)} %param.5), kind=kOutput, calls=%fused_computation.31 | convolution fusion | flops 4831838208 | bytes 9175040 | tf_op jit(solution)/shard_map/dot_general | solution.py:43
  25.7 33.4 %collective-permute-done.1 = f32[256,2048]{1,0:T(8,128)S(1)} collective-permute-done((f32[256,2048]{1,0:T(8,128)}, f32[256,2048]{1,0:T(8,128)S(1)}, u32[]{:S(2)}, u32[]{:S(2)}) %collective-permute-start.1) | collective-permute-done | bytes 2097184 | tf_op jit(solution)/shard_map/ppermute | solution.py:13
  59.1 0.0 copy-done.1
  59.1 5.1 fusion.42
  64.3 68.4 %collective-permute-done = f32[256,2048]{1,0:T(8,128)S(1)} collective-permute-done((f32[256,2048]{1,0:T(8,128)}, f32[256,2048]{1,0:T(8,128)S(1)}, u32[]{:S(2)}, u32[]{:S(2)}) %collective-permute-start) | collective-permute-done | bytes 2097184 | tf_op jit(solution)/shard_map/ppermute | solution.py:13
  132.7 5.3 fusion.45
  138.0 0.0 collective-permute-done.2
  138.0 7.8 %add_add_fusion = f32[768,2048]{1,0:T(8,128)} fusion(f32[768,2048]{1,0:T(8,128)S(1)} %fusion.42, f32[768,2048]{1,0:T(8,128)S(1)} %fusion.48, f32[768,2048]{1,0:T(8,128)S(1)} %fusion.45, f32[256,2048]{1,0:T(8,128)S(1)} %collective-permute-done.2, f32[1,4,768,256]{3,2,1,0:T(8,128)S(1)} %copy-done.1), kind=kOutput, calls=%fused_computation | convolution fusion | flops 4836556800 | bytes 28049408 | tf_op jit(solution)/shard_map/dot_general | solution.py:47
  145.8 0.0 reduce-scatter.2.cloned.1.call-update
  145.9 0.0 all-reduce.2.cloned.1.call-start
  145.9 32.8 %reduce-scatter.2.cloned.1.call-done = f32[384,2048]{1,0:T(8,128)} async-done(((f32[768,2048]{1,0:T(8,128)}), f32[384,2048]{1,0:T(8,128)}) %reduce-scatter.2.cloned.1.call-update) | async-done | bytes 3145744 | tf_op jit(solution)/shard_map/reduce_scatter | solution.py:26
  178.7 0.0 copy-start.2
  178.7 0.0 all-reduce.2.cloned.1.call-update
  178.7 0.0 all-gather.2.cloned.1.call-start
  178.8 166.7 %all-reduce.2.cloned.1.call-done = f32[384,2048]{1,0:T(8,128)} async-done(((f32[384,2048]{1,0:T(8,128)}), f32[384,2048]{1,0:T(8,128)}) %all-reduce.2.cloned.1.call-update) | async-done | bytes 3145744 | tf_op jit(solution)/shard_map/psum | solution.py:27
  345.4 0.0 all-gather.2.cloned.1.call-update
  346.1 0.0 copy-done.2
  346.2 20.5 %all-gather.2.cloned.1.call-done = f32[768,2048]{1,0:T(8,128)} async-done(((f32[384,2048]{1,0:T(8,128)}), f32[768,2048]{1,0:T(8,128)}) %all-gather.2.cloned.1.call-update) | async-done | bytes 6291472 | tf_op jit(solution)/shard_map/all_gather | solution.py:28
  366.7 0.0 copy-start
  366.7 12.4 %fusion.15 = f32[256,2048]{0,1:T(8,128)S(1)} fusion(f32[768,2048]{1,0:T(8,128)} %all-gather.2.cloned.1.call-done, f32[768]{0:T(1024)S(1)} %fusion.58, f32[1,4,768,256]{3,2,1,0:T(8,128)S(1)} %copy-done.1), kind=kOutput, calls=%fused_computation.14 | convolution fusion | flops 4833411072 | bytes 9179136 | tf_op jit(solution)/shard_map/dot_general | solution.py:58
  379.2 3.0 collective-permute-start.3
  382.1 0.0 copy-done
  382.1 10.4 %fusion.18 = f32[256,2048]{0,1:T(8,128)S(1)} fusion(f32[768,2048]{1,0:T(8,128)S(1)} %copy-done, f32[768]{0:T(1024)S(1)} %fusion.58, f32[1,4,768,256]{3,2,1,0:T(8,128)S(1)} %copy-done.1), kind=kOutput, calls=%fused_computation.15 | convolution fusion | flops 4833411072 | bytes 9179136 | tf_op jit(solution)/shard_map/dot_general | solution.py:58
  392.6 3.7 collective-permute-start.4
  396.3 10.4 %fusion.21 = f32[256,2048]{0,1:T(8,128)S(1)} fusion(f32[768,2048]{1,0:T(8,128)S(1)} %copy-done, f32[768]{0:T(1024)S(1)} %fusion.58, f32[1,4,768,256]{3,2,1,0:T(8,128)S(1)} %copy-done.1), kind=kOutput, calls=%fused_computation.16 | convolution fusion | flops 4833411072 | bytes 9179136 | tf_op jit(solution)/shard_map/dot_general | solution.py:58
  406.8 2.1 collective-permute-start.5
  408.9 88.0 %collective-permute-done.3 = f32[256,2048]{0,1:T(8,128)S(1)} collective-permute-done((f32[256,2048]{0,1:T(8,128)S(1)}, f32[256,2048]{0,1:T(8,128)S(1)}, u32[]{:S(2)}, u32[]{:S(2)}) %collective-permute-start.3) | collective-permute-done | bytes 2097184 | tf_op jit(solution)/shard_map/ppermute | solution.py:13
  496.9 0.0 collective-permute-done.4
  496.9 25.5 %collective-permute-done.5 = f32[256,2048]{0,1:T(8,128)S(1)} collective-permute-done((f32[256,2048]{0,1:T(8,128)S(1)}, f32[256,2048]{0,1:T(8,128)S(1)}, u32[]{:S(2)}, u32[]{:S(2)}) %collective-permute-start.5) | collective-permute-done | bytes 2097184 | tf_op jit(solution)/shard_map/ppermute | solution.py:13
  522.4 11.7 %fusion.33 = f32[1,256,2048]{1,2,0:T(8,128)} fusion(f32[256,2048]{0,1:T(8,128)S(1)} %collective-permute-done.5, f32[256,2048]{0,1:T(8,128)S(1)} %collective-permute-done.4, f32[256,2048]{0,1:T(8,128)S(1)} %collective-permute-done.3, f32[768,2048]{1,0:T(8,128)S(1)} %copy-done, f32[768]{0:T(1024)S(1)} %fusion.58, f32[1,4,768,256]{3,2,1,0:T(8,128)S(1)} %copy-done.1), kind=kOutput, calls=%fused_computation.20 | convolution fusion | flops 4834983936 | bytes 15470592 | tf_op jit(solution)/shard_map/dot_general | solution.py:58
  534.0 2.9 copy.5
  (2 shorter events, 0.0 us)
Async XLA Ops:
  6.5 172.2 %reduce-scatter.2.cloned.1.call-start = ((), (), s32[]{:S(2)}) async-start(), calls=%async_computation.1 | async-start | bytes 9437184 | tf_op jit(solution)/shard_map/reduce_scatter | solution.py:26
  6.5 52.6 %copy-start.1 = (f32[1,4,768,256]{3,2,1,0:T(8,128)S(1)}, f32[1,4,768,256]{3,2,1,0:T(8,128)}, u32[]{:S(2)}) copy-start(f32[1,4,768,256]{3,2,1,0:T(8,128)} %param.4) | copy-start | bytes 9437188
  6.5 52.6 %collective-permute-start.1 = (f32[256,2048]{1,0:T(8,128)}, f32[256,2048]{1,0:T(8,128)S(1)}, u32[]{:S(2)}, u32[]{:S(2)}) collective-permute-start(f32[256,2048]{1,0:T(8,128)} %bitcast.48), channel_id=1, source_target_pairs={{0,64},{32,96},{64,128},{96,160},{128,192},{160,224},{1,65},{33,97... | collective-permute-start | bytes 6291464 | tf_op jit(solution)/shard_map/ppermute | solution.py:13
  12.7 119.9 %collective-permute-start = (f32[256,2048]{1,0:T(8,128)}, f32[256,2048]{1,0:T(8,128)S(1)}, u32[]{:S(2)}, u32[]{:S(2)}) collective-permute-start(f32[256,2048]{1,0:T(8,128)} %bitcast.49), channel_id=1, source_target_pairs={{0,32},{32,64},{64,96},{96,128},{128,160},{160,192},{192,224},{1,3... | collective-permute-start | bytes 6291464 | tf_op jit(solution)/shard_map/ppermute | solution.py:13
  16.8 121.3 %collective-permute-start.2 = (f32[256,2048]{1,0:T(8,128)}, f32[256,2048]{1,0:T(8,128)S(1)}, u32[]{:S(2)}, u32[]{:S(2)}) collective-permute-start(f32[256,2048]{1,0:T(8,128)} %bitcast.50), channel_id=1, source_target_pairs={{0,96},{32,128},{64,160},{96,192},{128,224},{1,97},{33,129},{65,16... | collective-permute-start | bytes 6291464 | tf_op jit(solution)/shard_map/ppermute | solution.py:13
  145.9 199.6 %all-reduce.2.cloned.1.call-start = ((), (), s32[]{:S(2)}) async-start(), calls=%async_computation.2 | async-start | bytes 6291456 | tf_op jit(solution)/shard_map/psum | solution.py:27
  178.7 167.4 %copy-start.2 = (f32[1,768]{1,0:T(1,128)S(1)}, f32[1,768]{1,0:T(1,128)}, u32[]{:S(2)}) copy-start(f32[1,768]{1,0:T(1,128)} %param.6) | copy-start | bytes 9220
  178.7 188.0 %all-gather.2.cloned.1.call-start = ((), (), s32[]{:S(2)}) async-start(), calls=%async_computation.3 | async-start | bytes 9437184 | tf_op jit(solution)/shard_map/all_gather | solution.py:28
  366.7 15.4 %copy-start = (f32[768,2048]{1,0:T(8,128)S(1)}, f32[768,2048]{1,0:T(8,128)}, u32[]{:S(2)}) copy-start(f32[768,2048]{1,0:T(8,128)} %all-gather.2.cloned.1.call-done) | copy-start | bytes 18874372
  379.2 117.8 %collective-permute-start.3 = (f32[256,2048]{0,1:T(8,128)S(1)}, f32[256,2048]{0,1:T(8,128)S(1)}, u32[]{:S(2)}, u32[]{:S(2)}) collective-permute-start(f32[256,2048]{0,1:T(8,128)S(1)} %fusion.15), channel_id=1, source_target_pairs={{32,0},{64,32},{96,64},{128,96},{160,128},{192,160},{224,192},{33,... | collective-permute-start | bytes 6291464 | tf_op jit(solution)/shard_map/ppermute | solution.py:13
  392.6 104.3 %collective-permute-start.4 = (f32[256,2048]{0,1:T(8,128)S(1)}, f32[256,2048]{0,1:T(8,128)S(1)}, u32[]{:S(2)}, u32[]{:S(2)}) collective-permute-start(f32[256,2048]{0,1:T(8,128)S(1)} %fusion.18), channel_id=1, source_target_pairs={{64,0},{96,32},{128,64},{160,96},{192,128},{224,160},{65,1},{97,33... | collective-permute-start | bytes 6291464 | tf_op jit(solution)/shard_map/ppermute | solution.py:13
  406.8 115.6 %collective-permute-start.5 = (f32[256,2048]{0,1:T(8,128)S(1)}, f32[256,2048]{0,1:T(8,128)S(1)}, u32[]{:S(2)}, u32[]{:S(2)}) collective-permute-start(f32[256,2048]{0,1:T(8,128)S(1)} %fusion.21), channel_id=1, source_target_pairs={{96,0},{128,32},{160,64},{192,96},{224,128},{97,1},{129,33},{161,6... | collective-permute-start | bytes 6291464 | tf_op jit(solution)/shard_map/ppermute | solution.py:13
Sparse Core Ops, SparseCore 0:
  146.0 32.6 reduce-scatter.1
  181.4 164.0 all-reduce.1
  347.2 19.4 all-gather.1
where the time goes:
time: 553 us; the launch traced here: 544 us
  waiting for transfers between devices  435 us (79%)
  matrix products  70.3 us (13%)
  starting transfers between devices  21 us (4%)
  between operations  14.1 us (3%)
    ppermute x6, waiting for transfers between devices, from_behind(): return lax.ppermute(value, axis, pairs)  215 us
    psum x1, waiting for transfers between devices, nested_sum(): own = lax.psum(own, far)  167 us
    dot_general x4, matrix products, on_device(): lax.dot_general(foot_slab[lag_step], weighted, (((0,), (0,)), ((), ())),...  45 us
    reduce_scatter x1, waiting for transfers between devices, nested_sum(): own = lax.psum_scatter(padded, near, scatter_dimension=0, tiled=True)  32.8 us
    ppermute x6, starting transfers between devices, from_behind(): return lax.ppermute(value, axis, pairs)  20.9 us
    all_gather x1, waiting for transfers between devices, nested_sum(): whole = lax.all_gather(own, near, axis=0, tiled=True)  20.5 us
    dot_general x3, matrix products, on_device(): jnp.dot(foot_slab[lag_step], earlier[lag_step], precision=highest, prefer...  18.3 us
  transfers between devices with their start and end apart: 9, of which 7 were waited for; matrix products, arithmetic and copies ran while one was open for 7% of the time, Pallas kernels for 0%

commit v1 on v0

v1 whole, which is shorter than its diff:
```python
import functools

import jax
import jax.numpy as jnp
from jax import lax
from jax.experimental import pallas as pl
from jax.experimental.pallas import tpu as pltpu
from jax.sharding import PartitionSpec as P

MESH = pl.DeviceIdType.MESH
CHUNKS = 8
LAGS = 4

S1, S3, R2, X2, X1, SA, SB, GB, GA, D2, D1, D3, E1, E2, SC = range(15)
H1, H2, H3 = S1, R2, S3


def split(value):
    high = value.astype(jnp.bfloat16)
    low = (value - high.astype(jnp.float32)).astype(jnp.bfloat16)
    return high, low


def kernel(
    foot, flux, scale, out,
    hal, part, got_a, got_b, got_c, full, adj, in1, in2, in3, in_a, in_b,
    h_hi, h_lo, t_hi, t_lo, f_hi, f_lo, w_hi, w_lo, send, recv,
):
    chunks, rows, width = part.shape
    deep = flux.shape[0]
    t = lax.axis_index("tm")
    place = lax.axis_index("cells")
    nz = lax.axis_size("cells") // 4
    tsize = lax.axis_size("tm")
    gz = nz - 1
    x = lax.rem(t, 4)
    z = place // 4
    y = lax.rem(place // 2, 2)
    core = lax.rem(place, 2)
    half, quarter, piece = rows // 2, rows // 4, rows // (4 * nz)
    other_core = z * 4 + y * 2 + (1 - core)
    other_y = z * 4 + (1 - y) * 2 + core

    def z_peer(step):
        return lax.rem(z + step, nz) * 4 + y * 2 + core

    def z_from(step):
        return lax.rem(z + nz - step, nz)

    barrier = pltpu.get_barrier_semaphore()
    for by in (1, 3, tsize - 1, tsize - 3):
        pl.semaphore_signal(barrier, inc=1, device_id=(lax.rem(t + by, tsize), place), device_id_type=MESH)
    for who in [other_core, other_y] + [z_peer(s) for s in range(1, nz)]:
        pl.semaphore_signal(barrier, inc=1, device_id=(t, who), device_id_type=MESH)
    pl.semaphore_wait(barrier, 4 + 2 + gz)

    def copy(src, dst, kind, c, to_t, to_place, into=None):
        into = kind if into is None else into
        return pltpu.make_async_remote_copy(
            src_ref=src, dst_ref=dst, send_sem=send.at[kind, c], recv_sem=recv.at[into, c],
            device_id=(to_t, to_place), device_id_type=MESH,
        )

    def cols(c):
        return pl.ds(pl.multiple_of(c * width, width), width)

    def own(c):
        return flux.at[:, cols(c)]

    def down(by):
        return lax.rem(t + by, tsize)

    def row(start, size):
        return pl.ds(pl.multiple_of(start, 8), size)

    mine_y = core * half + y * quarter
    theirs_y = core * half + (1 - y) * quarter
    mine_z = mine_y + z * piece

    cp = {
        S1: (x != 3, lambda c: copy(own(c), hal.at[0, c], S1, c, down(1), place)),
        S3: (t <= 4, lambda c: copy(own(c), hal.at[2, c], S3, c, down(3), place)),
        R2: ((x == 1) | (x == 2), lambda c: copy(hal.at[0, c], hal.at[1, c], R2, c, down(1), place)),
        X2: ((t == 5) | (t == 6), lambda c: copy(hal.at[2, c], hal.at[1, c], X2, c, down(tsize - 1), place, R2)),
        X1: (t == 5, lambda c: copy(hal.at[1, c], hal.at[0, c], X1, c, down(tsize - 1), place, S1)),
        SA: (None, lambda c: copy(part.at[c, row((1 - core) * half, half)], got_a.at[c], SA, c, t, other_core)),
        SB: (None, lambda c: copy(part.at[c, row(theirs_y, quarter)], got_b.at[c], SB, c, t, other_y)),
        GB: (None, lambda c: copy(full.at[c, row(mine_y, quarter)], full.at[c, row(mine_y, quarter)], GB, c, t, other_y)),
        GA: (None, lambda c: copy(full.at[c, row(core * half, half)], full.at[c, row(core * half, half)], GA, c, t, other_core)),
        D2: (x >= 2, lambda c: copy(adj.at[1, c], in2.at[c], D2, c, down(tsize - 1), place)),
        D1: (x >= 1, lambda c: copy(adj.at[0, c], in1.at[c], D1, c, down(tsize - 1), place)),
        D3: (t >= 3, lambda c: copy(adj.at[2, c], in3.at[c], D3, c, down(tsize - 3), place)),
        E1: ((t == 4) | (t == 5), lambda c: copy(adj.at[t - 4, c], in_a.at[c], E1, c, down(1), place)),
        E2: (t == 4, lambda c: copy(adj.at[1, c], in_b.at[c], E2, c, down(1), place)),
    }

    def c_send(step, c):
        to = lax.rem(z + step, nz)
        return copy(part.at[c, row(mine_y + to * piece, piece)], got_c.at[c, step - 1], SC + step - 1, c, t, z_peer(step))

    def c_gather(step, c):
        return copy(full.at[c, row(mine_z, piece)], full.at[c, row(mine_z, piece)], SC + gz + step - 1, c, t, z_peer(step))

    def start(kind, c, when=None):
        cond = cp[kind][0] if when is None else when
        if cond is None:
            cp[kind][1](c).start()
        else:
            pl.when(cond)(lambda: cp[kind][1](c).start())

    def landed(ref, kind, c, when=None):
        def wait():
            copy(ref, ref, kind, c, t, other_core).wait_recv()

        if when is None:
            wait()
        else:
            pl.when(when)(wait)

    relays_1 = (x == 1) | (x == 2)
    relays_3 = (t == 5) | (t == 6)

    def own_sends(c):
        start(S3, c)
        start(S1, c)

    def relay_1(c):
        landed(hal.at[0, c], H1, c, relays_1)
        start(R2, c)
        landed(hal.at[2, c], H3, c, relays_3)
        start(X2, c)

    def relay_2(c):
        landed(hal.at[1, c], H2, c, t == 5)
        start(X1, c)

    def forward(c):
        landed(hal.at[0, c], H1, c, (t >= 1) & ~relays_1)
        landed(hal.at[1, c], H2, c, (t >= 2) & (t != 5))
        landed(hal.at[2, c], H3, c, (t >= 3) & ~relays_3)
        for lag in range(LAGS):
            value = flux[:, cols(c)] if lag == 0 else hal[lag - 1, c]
            high, low = split(value)
            f_hi[lag * deep : (lag + 1) * deep, :] = high
            f_lo[lag * deep : (lag + 1) * deep, :] = low

        tile = rows // 4

        def block(m, carry):
            at = pl.ds(pl.multiple_of(m * tile, 8), tile)
            hh, hl = h_hi[at, :], h_lo[at, :]
            total = jnp.dot(hh, f_hi[...], preferred_element_type=jnp.float32)
            total = total + jnp.dot(hh, f_lo[...], preferred_element_type=jnp.float32)
            total = total + jnp.dot(hl, f_hi[...], preferred_element_type=jnp.float32)
            part[c, at, :] = total
            return carry

        lax.fori_loop(0, 4, block, 0)
        start(SA, c)

    def sum_a(c):
        landed(got_a.at[c], SA, c)
        at = row(core * half, half)
        part[c, at, :] = part[c, at, :] + got_a[c]
        start(SB, c)

    def sum_b(c):
        landed(got_b.at[c], SB, c)
        at = row(mine_y, quarter)
        part[c, at, :] = part[c, at, :] + got_b[c]
        for step in range(1, nz):
            c_send(step, c).start()

    def sum_c(c):
        total = part[c, row(mine_z, piece), :]
        for step in range(1, nz):
            landed(got_c.at[c, step - 1], SC + step - 1, c)
            total = total + got_c[c, step - 1]
        full[c, row(mine_z, piece), :] = total * scale[:, 0:1]
        for step in range(1, nz):
            c_gather(step, c).start()

    def gather_b(c):
        for step in range(1, nz):
            landed(full.at[c, row(mine_y + z_from(step) * piece, piece)], SC + gz + step - 1, c)
        start(GB, c)

    def gather_a(c):
        landed(full.at[c, row(theirs_y, quarter)], GB, c)
        start(GA, c)

    def adjoint(c):
        landed(full.at[c, row((1 - core) * half, half)], GA, c)
        high, low = split(full[c])
        w_hi[...] = high
        w_lo[...] = low

        def block(lag):
            at = pl.ds(lag * deep, deep)
            hh, hl = t_hi[at, :], t_lo[at, :]
            total = jnp.dot(hh, w_hi[...], preferred_element_type=jnp.float32)
            total = total + jnp.dot(hh, w_lo[...], preferred_element_type=jnp.float32)
            return total + jnp.dot(hl, w_hi[...], preferred_element_type=jnp.float32)

        adj[2, c] = block(3)
        adj[1, c] = block(2)
        start(D2, c)
        start(E2, c)
        start(D3, c, (t == 3) | (t == 4) | (t == 7))
        adj[0, c] = block(1)
        start(E1, c, t == 4)
        start(D1, c, x == 3)
        out[:, cols(c)] = block(0)

    def back_1(c):
        @pl.when(t == 5)
        def _():
            landed(in_a.at[c], E1, c)
            adj[1, c] = adj[1, c] + in_a[c]
            start(E1, c, t == 5)
            landed(in_b.at[c], E2, c)
            adj[2, c] = adj[2, c] + in_b[c]
            start(D3, c, t == 5)

        @pl.when(relays_1)
        def _():
            landed(in2.at[c], D2, c)
            adj[0, c] = adj[0, c] + in2[c]
            start(D1, c, x <= 2)

    def back_2(c):
        @pl.when(t == 6)
        def _():
            landed(in_a.at[c], E1, c)
            adj[2, c] = adj[2, c] + in_a[c]
            start(D3, c, t == 6)

    def finish(c):
        @pl.when(x <= 2)
        def _():
            landed(in1.at[c], D1, c)
            out[:, cols(c)] = out[:, cols(c)] + in1[c]

        @pl.when(t <= 4)
        def _():
            landed(in3.at[c], D3, c)
            out[:, cols(c)] = out[:, cols(c)] + in3[c]

    order = [
        (own_sends, -3),
        (relay_1, -2),
        (relay_2, -1),
        (forward, 0),
        (gather_a, 2),
        (sum_c, 1),
        (adjoint, 2),
        (sum_a, 0),
        (back_2, 3),
        (sum_b, 0),
        (gather_b, 1),
        (finish, 3),
        (back_1, 2),
    ]
    first, last = min(d for _, d in order), max(d for _, d in order)

    def step(i, carry):
        for stage, delay in order:
            c = i - delay
            pl.when((c >= 0) & (c < chunks))(functools.partial(stage, c))
        return carry

    def prepare(lag, carry):
        value = foot[lag]
        at = pl.ds(pl.multiple_of(lag * deep, deep), deep)
        h_hi[:, at], h_lo[:, at] = split(value)
        t_hi[at, :], t_lo[at, :] = split(value.T)
        return carry

    lead = 3
    for c in range(lead):
        own_sends(c)
    lax.fori_loop(0, LAGS, prepare, 0)
    for lag in range(1, LAGS):

        @pl.when(t < lag)
        def _(lag=lag):
            hal[lag - 1] = jnp.zeros(hal.shape[1:], hal.dtype)

    order[0] = (lambda c: pl.when(c >= lead)(functools.partial(own_sends, c)), order[0][1])
    lax.fori_loop(first, chunks + last, step, 0)

    def drain(c, carry):
        for kind, (cond, make) in cp.items():
            if cond is None:
                make(c).wait_send()
            else:
                pl.when(cond)(lambda make=make: make(c).wait_send())
        for s in range(1, nz):
            c_send(s, c).wait_send()
            c_gather(s, c).wait_send()
        return carry

    lax.fori_loop(0, chunks, drain, 0)


def on_device(footprint, flux, obs_weight, obs_count):
    lags, slots, deep = footprint.shape[1:]
    wide = flux.shape[2]
    chunks = CHUNKS
    width = wide // chunks
    nz = lax.axis_size("cells") // 4
    piece = slots // (4 * nz)
    place = lax.axis_index("cells")
    base = lax.rem(place, 2) * (slots // 2) + lax.rem(place // 2, 2) * (slots // 4) + (place // 4) * piece
    mine = base + jnp.arange(piece, dtype=jnp.int32)
    weight = lax.dynamic_slice(obs_weight[0], (base,), (piece,))
    row_scale = jnp.where(mine < obs_count[0], weight, 0.0)
    scale = jnp.broadcast_to(row_scale[:, None], (piece, 128))
    f32, bf16 = jnp.float32, jnp.bfloat16
    wide_block = pltpu.VMEM((chunks, deep, width), f32)
    kinds = SC + 2 * (nz - 1)
    result = pl.pallas_call(
        kernel,
        out_shape=jax.ShapeDtypeStruct((deep, wide), f32),
        in_specs=[pl.BlockSpec(memory_space=pltpu.VMEM)] * 3,
        out_specs=pl.BlockSpec(memory_space=pltpu.VMEM),
        scratch_shapes=[
            pltpu.VMEM((lags - 1, chunks, deep, width), f32),
            pltpu.VMEM((chunks, slots, width), f32),
            pltpu.VMEM((chunks, slots // 2, width), f32),
            pltpu.VMEM((chunks, slots // 4, width), f32),
            pltpu.VMEM((chunks, nz - 1, piece, width), f32),
            pltpu.VMEM((chunks, slots, width), f32),
            pltpu.VMEM((lags - 1, chunks, deep, width), f32),
            wide_block,
            wide_block,
            wide_block,
            wide_block,
            wide_block,
            pltpu.VMEM((slots, lags * deep), bf16),
            pltpu.VMEM((slots, lags * deep), bf16),
            pltpu.VMEM((lags * deep, slots), bf16),
            pltpu.VMEM((lags * deep, slots), bf16),
            pltpu.VMEM((lags * deep, width), bf16),
            pltpu.VMEM((lags * deep, width), bf16),
            pltpu.VMEM((slots, width), bf16),
            pltpu.VMEM((slots, width), bf16),
            pltpu.SemaphoreType.DMA((kinds, chunks)),
            pltpu.SemaphoreType.DMA((kinds, chunks)),
        ],
        compiler_params=pltpu.CompilerParams(
            collective_id=0, has_side_effects=True, vmem_limit_bytes=67043328
        ),
    )(footprint[0], flux[0], scale)
    return result[None]


def solution(mesh):
    placed = (P("tm", None, None, "cells"), P("tm", "cells", None), P("tm", None), P("tm"))
    return jax.shard_map(
        on_device, mesh=mesh, in_specs=placed, out_specs=P("tm", "cells", None), check_vma=False
    )
```

time: 553 us -> 253 us (0.46); the launches traced: 544 us -> 252 us
  waiting for transfers between devices: 435 us -> 0 us
  Pallas kernels: 0 us -> 247 us
  matrix products: 70.3 us -> 0 us
  starting transfers between devices: 21 us -> 0 us
  between operations: 14.1 us -> 0.66 us
    pallas_call x0 -> x1, Pallas kernels: none -> 247 us  [on_device(): pl.pallas_call(kernel, out_shape=jax.ShapeDtypeStruct((deep, wide), f32),...]
    ppermute x6 -> x0, waiting for transfers between devices: 215 us -> none  [from_behind(): return lax.ppermute(value, axis, pairs)]
    psum x1 -> x0, waiting for transfers between devices: 167 us -> none  [nested_sum(): own = lax.psum(own, far)]
    dot_general x8 -> x0, matrix products: 70.3 us -> none  [the longest x4 45 us: on_device(): lax.dot_general(foot_slab[lag_step], weighted, (((0,), (0,)), ((), ())),...]
    reduce_scatter x1 -> x0, waiting for transfers between devices: 32.8 us -> none  [nested_sum(): own = lax.psum_scatter(padded, near, scatter_dimension=0, tiled=True)]
    ppermute x6 -> x0, starting transfers between devices: 20.9 us -> none  [from_behind(): return lax.ppermute(value, axis, pairs)]
    all_gather x1 -> x0, waiting for transfers between devices: 20.5 us -> none  [nested_sum(): whole = lax.all_gather(own, near, axis=0, tiled=True)]
  transfers between devices with their start and end apart: 9 -> 0, of which waited for: 7 -> 0; matrix products, arithmetic and copies ran while one was open for 7% -> 0% of each run, Pallas kernels for 0% -> 0%
where the time goes in v1:
time: 253 us; the launch traced here: 252 us
  Pallas kernels  247 us (98%)
  local copies, waits for them, and re-layouts  3.81 us (2%)
    pallas_call x1, Pallas kernels, on_device(): pl.pallas_call(kernel, out_shape=jax.ShapeDtypeStruct((deep, wide), f32),...  247 us

profile of v1, /device:TPU:6, one launch (start us, length us, event | category | flops | bytes accessed | tf_op | source)
XLA Modules:
  0.0 252.1 jit_solution(15364345155948447208)
XLA Ops:
  0.7 0.8 compare_select_fusion
  1.4 0.7 broadcast_in_dim.14.scale
  2.1 246.9 %shard_map.46 = f32[256,2048]{1,0:T(8,128)} custom-call(f32[4,768,256]{2,1,0:T(8,128)} %bitcast.8, f32[256,2048]{1,0:T(8,128)} %bitcast.9, f32[24,128]{1,0:T(8,128)} %broadcast_in_dim.14.scale), custom_call_target="tpu_custom_call" | custom-call | tf_op jit(solution)/shard_map/pallas_call | solution.py:322
  249.0 3.1 %copy.7 = f32[1,256,2048]{2,1,0:T(8,128)} copy(f32[1,256,2048]{2,1,0:T(8,128)} %bitcast.7) | data formatting | bytes 4194304

commit v2 on v1

v2 whole, which is shorter than its diff:
```python
import functools

import jax
import jax.numpy as jnp
from jax import lax
from jax.experimental import pallas as pl
from jax.experimental.pallas import tpu as pltpu
from jax.sharding import PartitionSpec as P

MESH = pl.DeviceIdType.MESH
CHUNKS = 8
LEAD = 2
ORDER = [("late_sends", -3), ("late_relay", -2), ("forward", 0), ("turn", 0), ("adjoint", 4), ("sum_3", 2), ("sum_2", 1), ("relay_2", -1), ("back_2", 5), ("sum_1", 0), ("gather_2", 3), ("finish", 7), ("gather_1", 2), ("back_1", 4), ("cross_1", 5)]
LAGS = 4

S1, S3, Y3, R2, X2, Z1, Z3, P0, P2, P4, SA, SB, TB, GB, HB, GA, D2, D1, D3, E1, E2, E3, F1, V3, W3, SC = range(26)
H1, H2, H3 = S1, R2, S3


def split(value):
    high = value.astype(jnp.bfloat16)
    low = (value - high.astype(jnp.float32)).astype(jnp.bfloat16)
    return high, low


def kernel(
    foot, flux, scale, out,
    hal, part, got_a, got_b, got_c, full, adj, in1, in2, in3, in_a, in_b,
    h_hi, h_lo, t_hi, t_lo, f_hi, f_lo, w_hi, w_lo, send, recv,
):
    chunks, rows, width = part.shape
    deep = flux.shape[0]
    t = lax.axis_index("tm")
    place = lax.axis_index("cells")
    nz = lax.axis_size("cells") // 4
    tsize = lax.axis_size("tm")
    gz = nz - 1
    x = lax.rem(t, 4)
    z = place // 4
    y = lax.rem(place // 2, 2)
    core = lax.rem(place, 2)
    half, quarter, piece = rows // 2, rows // 4, rows // (4 * nz)
    other_core = z * 4 + y * 2 + (1 - core)
    other_y = z * 4 + (1 - y) * 2 + core

    def z_peer(step):
        return lax.rem(z + step, nz) * 4 + y * 2 + core

    def z_from(step):
        return lax.rem(z + nz - step, nz)

    barrier = pltpu.get_barrier_semaphore()
    for by in (1, 3, 4, tsize - 1, tsize - 3):
        pl.semaphore_signal(barrier, inc=1, device_id=(lax.rem(t + by, tsize), place), device_id_type=MESH)
    for by in (1, 4, tsize - 1):
        pl.semaphore_signal(barrier, inc=1, device_id=(lax.rem(t + by, tsize), other_y), device_id_type=MESH)
    for who in [other_core, other_y] + [z_peer(s) for s in range(1, nz)]:
        pl.semaphore_signal(barrier, inc=1, device_id=(t, who), device_id_type=MESH)
    pl.semaphore_wait(barrier, 5 + 3 + 2 + gz)

    def copy(src, dst, kind, c, to_t, to_place, into=None):
        into = kind if into is None else into
        return pltpu.make_async_remote_copy(
            src_ref=src, dst_ref=dst, send_sem=send.at[kind, c], recv_sem=recv.at[into, c],
            device_id=(to_t, to_place), device_id_type=MESH,
        )

    def cols(c):
        return pl.ds(pl.multiple_of(c * width, width), width)

    def own(c):
        return flux.at[:, cols(c)]

    def down(by):
        return lax.rem(t + by, tsize)

    def row(start, size):
        return pl.ds(pl.multiple_of(start, 8), size)

    first = core == 0
    top = core * half
    pair = 2 * piece
    mine = jnp.where(first, top + y * quarter + z * piece, top + z * pair + y * piece)
    over_y = jnp.where(first, mine, top + z * pair + (1 - y) * piece)
    mine_y = top + y * quarter
    theirs_y = top + (1 - y) * quarter
    mine_z = top + z * pair
    sides = ((first, piece, mine_y), (~first, pair, top))

    relays_1 = (x == 1) | (x == 2)
    relays_3 = (t == 5) | (t == 6) | ((x == 3) & ~first)

    cp = {
        S1: (x != 3, lambda c: copy(own(c), hal.at[0, c], S1, c, down(1), place)),
        S3: ((t == 0) | ((t == 1) & first) | (t == 2) | (t == 4), lambda c: copy(own(c), hal.at[2, c], S3, c, down(3), place)),
        R2: (relays_1 & first, lambda c: copy(hal.at[0, c], hal.at[1, c], R2, c, down(1), place)),
        X2: (relays_3, lambda c: copy(hal.at[2, c], hal.at[1, c], X2, c, down(tsize - 1), place, R2)),
        Y3: (t == 3, lambda c: copy(own(c), in3.at[c], Y3, c, down(4), place)),
        P0: (((t == 1) | (t == 5)) & ~first, lambda c: copy(own(c), in2.at[c], P0, c, down(tsize - 1), place)),
        P2: ((x == 0) & ~first, lambda c: copy(in2.at[c], hal.at[1, c], P2, c, down(3), place, R2)),
        P4: ((t == 0) & ~first, lambda c: copy(in2.at[c], hal.at[2, c], P4, c, down(4), place, S3)),
        Z1: (t == 7, lambda c: copy(in3.at[c], hal.at[0, c], Z1, c, down(tsize - 3), place, S1)),
        Z3: (t == 7, lambda c: copy(in3.at[c], hal.at[2, c], Z3, c, down(tsize - 1), place, S3)),
        SA: (None, lambda c: copy(part.at[c, row((1 - core) * half, half)], got_a.at[c], SA, c, t, other_core)),
        SB: (first, lambda c: copy(part.at[c, row(theirs_y, quarter)], got_b.at[c], SB, c, t, other_y)),
        TB: (~first, lambda c: copy(part.at[c, row(over_y, piece)], got_b.at[c, 0:piece], TB, c, t, other_y, SB)),
        GB: (first, lambda c: copy(full.at[c, row(mine_y, quarter)], full.at[c, row(mine_y, quarter)], GB, c, t, other_y)),
        HB: (~first, lambda c: copy(full.at[c, row(mine, piece)], full.at[c, row(mine, piece)], HB, c, t, other_y, GB)),
        GA: (None, lambda c: copy(full.at[c, row(core * half, half)], full.at[c, row(core * half, half)], GA, c, t, other_core)),
        D2: (x >= 2, lambda c: copy(adj.at[1, c], in2.at[c], D2, c, down(tsize - 1), place)),
        D1: (x >= 1, lambda c: copy(adj.at[0, c], in1.at[c], D1, c, down(tsize - 1), place)),
        D3: (x == 3, lambda c: copy(adj.at[2, c], in3.at[c], D3, c, down(tsize - 3), place)),
        F1: (t == 7, lambda c: copy(in_a.at[c], in3.at[c], F1, c, down(tsize - 4), place, D3)),
        V3: ((t == 4) | (t == 5), lambda c: copy(adj.at[2, c], in_a.at[c], V3, c, down(tsize - 4), other_y)),
        W3: (t <= 1, lambda c: copy(in_a.at[c], in3.at[c], W3, c, down(1), other_y, D3)),
        E1: ((t == 5) | (t == 6), lambda c: copy(adj.at[t - 4, c], in_a.at[c], E1, c, down(1), place)),
        E2: (t == 4, lambda c: copy(adj.at[1, c], in_b.at[c], E2, c, down(1), place)),
        E3: (t == 4, lambda c: copy(adj.at[0, c], in_b.at[c], E3, c, down(3), place, E2)),
    }

    def c_send(step, c, size, base):
        to = lax.rem(z + step, nz)
        return copy(part.at[c, row(base + to * size, size)], got_c.at[c, step - 1, 0:size], SC + step - 1, c, t, z_peer(step))

    def c_gather(step, c, size, base):
        at = row(base + z * size, size)
        return copy(full.at[c, at], full.at[c, at], SC + gz + step - 1, c, t, z_peer(step))

    def start(kind, c, when=None):
        cond = cp[kind][0] if when is None else when
        if cond is None or cond is True:
            cp[kind][1](c).start()
        else:
            pl.when(cond)(lambda: cp[kind][1](c).start())

    def landed(ref, kind, c, when=None):
        def wait():
            copy(ref, ref, kind, c, t, other_core).wait_recv()

        if when is None:
            wait()
        else:
            pl.when(when)(wait)

    def own_sends(c):
        start(Y3, c)
        start(P0, c)
        start(S3, c)
        start(S1, c)

    def relay_1(c):
        @pl.when(t == 7)
        def _():
            landed(in3.at[c], Y3, c)
            start(Z1, c, True)
            start(Z3, c, True)

        @pl.when((x == 0) & ~first)
        def _():
            landed(in2.at[c], P0, c)
            start(P2, c, True)
            start(P4, c, t == 0)

        early = relays_3 & (t != 6)
        landed(hal.at[2, c], H3, c, early)
        start(X2, c, early)
        landed(hal.at[0, c], H1, c, relays_1 & first)
        start(R2, c)

    def relay_2(c):
        landed(hal.at[2, c], H3, c, t == 6)
        start(X2, c, t == 6)

    def forward(c):
        landed(hal.at[0, c], H1, c, (t >= 1) & ~(relays_1 & first))
        landed(hal.at[1, c], H2, c, t >= 2)
        landed(hal.at[2, c], H3, c, (t >= 3) & ~relays_3)
        for lag in range(LAGS):
            value = flux[:, cols(c)] if lag == 0 else hal[lag - 1, c]
            high, low = split(value)
            f_hi[lag * deep : (lag + 1) * deep, :] = high
            f_lo[lag * deep : (lag + 1) * deep, :] = low

        tile = rows // 4

        def block(m, carry):
            at = pl.ds(pl.multiple_of(m * tile, 8), tile)
            hh, hl = h_hi[at, :], h_lo[at, :]
            total = jnp.dot(hh, f_hi[...], preferred_element_type=jnp.float32)
            total = total + jnp.dot(hh, f_lo[...], preferred_element_type=jnp.float32)
            total = total + jnp.dot(hl, f_hi[...], preferred_element_type=jnp.float32)
            part[c, at, :] = total
            return carry

        lax.fori_loop(0, 4, block, 0)
        start(SA, c)

    def spread(c, size, base):
        for step in range(1, nz):
            c_send(step, c, size, base).start()

    def collect(c, size, base):
        at = row(base + z * size, size)
        total = part[c, at, :]
        for step in range(1, nz):
            landed(got_c.at[c, step - 1, 0:size], SC + step - 1, c)
            total = total + got_c[c, step - 1, 0:size, :]
        return at, total

    def share(c, size, base):
        for step in range(1, nz):
            c_gather(step, c, size, base).start()

    def shared(c, size, base):
        for step in range(1, nz):
            landed(full.at[c, row(base + z_from(step) * size, size)], SC + gz + step - 1, c)

    def sum_1(c):
        landed(got_a.at[c], SA, c)
        at = row(top, half)
        part[c, at, :] = part[c, at, :] + got_a[c]
        start(SB, c)
        pl.when(~first)(lambda: spread(c, pair, top))

    def sum_2(c):
        @pl.when(first)
        def _():
            landed(got_b.at[c], SB, c)
            at = row(mine_y, quarter)
            part[c, at, :] = part[c, at, :] + got_b[c]
            spread(c, piece, mine_y)

        @pl.when(~first)
        def _():
            at, total = collect(c, pair, top)
            part[c, at, :] = total
            start(TB, c, True)

    def sum_3(c):
        @pl.when(first)
        def _():
            at, total = collect(c, piece, mine_y)
            full[c, at, :] = total * scale[:, 0:1]
            share(c, piece, mine_y)

        @pl.when(~first)
        def _():
            landed(got_b.at[c, 0:piece], SB, c)
            at = row(mine, piece)
            full[c, at, :] = (part[c, at, :] + got_b[c, 0:piece]) * scale[:, 0:1]
            start(HB, c, True)

    def gather_1(c):
        @pl.when(first)
        def _():
            shared(c, piece, mine_y)
            start(GB, c, True)

        @pl.when(~first)
        def _():
            landed(full.at[c, row(over_y, piece)], GB, c)
            share(c, pair, top)

    def gather_2(c):
        landed(full.at[c, row(theirs_y, quarter)], GB, c, first)
        pl.when(~first)(lambda: shared(c, pair, top))
        start(GA, c)

    def adjoint(c):
        landed(full.at[c, row((1 - core) * half, half)], GA, c)
        high, low = split(full[c])
        w_hi[...] = high
        w_lo[...] = low

        def block(lag):
            at = pl.ds(lag * deep, deep)
            hh, hl = t_hi[at, :], t_lo[at, :]
            total = jnp.dot(hh, w_hi[...], preferred_element_type=jnp.float32)
            total = total + jnp.dot(hh, w_lo[...], preferred_element_type=jnp.float32)
            return total + jnp.dot(hl, w_hi[...], preferred_element_type=jnp.float32)

        adj[2, c] = block(3)
        adj[1, c] = block(2)
        start(D2, c)
        start(E2, c)
        start(E1, c, t == 5)
        start(D3, c)
        start(V3, c, t == 4)
        adj[0, c] = block(1)
        start(E3, c)
        start(D1, c, x == 3)
        out[:, cols(c)] = block(0)

    def back_1(c):
        @pl.when(t == 6)
        def _():
            landed(in_a.at[c], E1, c)
            adj[2, c] = adj[2, c] + in_a[c]
            start(E1, c, True)

        @pl.when(t == 5)
        def _():
            landed(in_b.at[c], E2, c)
            adj[2, c] = adj[2, c] + in_b[c]
            start(V3, c, True)

        @pl.when(relays_1)
        def _():
            landed(in2.at[c], D2, c)
            adj[0, c] = adj[0, c] + in2[c]
            start(D1, c, True)

    def back_2(c):
        @pl.when(t == 7)
        def _():
            landed(in_b.at[c], E2, c)
            landed(in_a.at[c], E1, c)
            in_a[c] = in_a[c] + in_b[c]
            start(F1, c, True)

    def cross_1(c):
        landed(in_a.at[c], V3, c, t <= 1)
        start(W3, c)

    def finish(c):
        @pl.when(x <= 2)
        def _():
            landed(in1.at[c], D1, c)
            out[:, cols(c)] = out[:, cols(c)] + in1[c]

        @pl.when(t <= 4)
        def _():
            landed(in3.at[c], D3, c)
            out[:, cols(c)] = out[:, cols(c)] + in3[c]

    def split_rows(lag):
        at = pl.ds(lag * deep, deep)
        h_hi[:, at], h_lo[:, at] = split(foot[lag])

    def split_turned(lag):
        at = pl.ds(lag * deep, deep)
        t_hi[at, :], t_lo[at, :] = split(foot[lag].T)

    def late_sends(c):
        pl.when(c >= LEAD)(lambda: own_sends(c))

    for c in range(LEAD):
        own_sends(c)
    split_rows(0)
    split_rows(1)
    relay_1(0)
    split_rows(2)
    split_rows(3)
    for lag in range(1, LAGS):

        @pl.when(t < lag)
        def _(lag=lag):
            hal[lag - 1] = jnp.zeros(hal.shape[1:], hal.dtype)

    def late_relay(c):
        pl.when(c >= 1)(lambda: relay_1(c))

    def turn(c):
        @pl.when(c == 0)
        def _():
            for lag in range(LAGS):
                split_turned(lag)

    named = locals()
    order = [(named[name], delay) for name, delay in ORDER]
    begin, end = min(d for _, d in order), max(d for _, d in order)

    def step(i, carry):
        for stage, delay in order:
            c = i - delay
            @pl.when((c >= 0) & (c < chunks))
            def _(stage=stage, c=c):
                with jax.named_scope(stage.__name__):
                    stage(c)
        return carry

    lax.fori_loop(begin, chunks + end, step, 0)

    def drain(c, carry):
        for kind, (cond, make) in cp.items():
            if cond is None:
                make(c).wait_send()
            else:
                pl.when(cond)(lambda make=make: make(c).wait_send())
        for cond, size, base in sides:

            @pl.when(cond)
            def _(size=size, base=base):
                for s in range(1, nz):
                    c_send(s, c, size, base).wait_send()
                    c_gather(s, c, size, base).wait_send()

        return carry

    lax.fori_loop(0, chunks, drain, 0)


def on_device(footprint, flux, obs_weight, obs_count):
    lags, slots, deep = footprint.shape[1:]
    wide = flux.shape[2]
    chunks = CHUNKS
    width = wide // chunks
    nz = lax.axis_size("cells") // 4
    piece = slots // (4 * nz)
    place = lax.axis_index("cells")
    core, y, z = lax.rem(place, 2), lax.rem(place // 2, 2), place // 4
    inner = jnp.where(core == 0, y * (slots // 4) + z * piece, (2 * z + y) * piece)
    base = core * (slots // 2) + inner
    mine = base + jnp.arange(piece, dtype=jnp.int32)
    weight = lax.dynamic_slice(obs_weight[0], (base,), (piece,))
    row_scale = jnp.where(mine < obs_count[0], weight, 0.0)
    scale = jnp.broadcast_to(row_scale[:, None], (piece, 128))
    f32, bf16 = jnp.float32, jnp.bfloat16
    wide_block = pltpu.VMEM((chunks, deep, width), f32)
    kinds = SC + 2 * (nz - 1)
    result = pl.pallas_call(
        kernel,
        out_shape=jax.ShapeDtypeStruct((deep, wide), f32),
        in_specs=[pl.BlockSpec(memory_space=pltpu.VMEM)] * 3,
        out_specs=pl.BlockSpec(memory_space=pltpu.VMEM),
        scratch_shapes=[
            pltpu.VMEM((lags - 1, chunks, deep, width), f32),
            pltpu.VMEM((chunks, slots, width), f32),
            pltpu.VMEM((chunks, slots // 2, width), f32),
            pltpu.VMEM((chunks, slots // 4, width), f32),
            pltpu.VMEM((chunks, nz - 1, 2 * piece, width), f32),
            pltpu.VMEM((chunks, slots, width), f32),
            pltpu.VMEM((lags - 1, chunks, deep, width), f32),
            wide_block,
            wide_block,
            wide_block,
            wide_block,
            wide_block,
            pltpu.VMEM((slots, lags * deep), bf16),
            pltpu.VMEM((slots, lags * deep), bf16),
            pltpu.VMEM((lags * deep, slots), bf16),
            pltpu.VMEM((lags * deep, slots), bf16),
            pltpu.VMEM((lags * deep, width), bf16),
            pltpu.VMEM((lags * deep, width), bf16),
            pltpu.VMEM((slots, width), bf16),
            pltpu.VMEM((slots, width), bf16),
            pltpu.SemaphoreType.DMA((kinds, chunks)),
            pltpu.SemaphoreType.DMA((kinds, chunks)),
        ],
        compiler_params=pltpu.CompilerParams(
            collective_id=0, has_side_effects=True, vmem_limit_bytes=67043328
        ),
    )(footprint[0], flux[0], scale)
    return result[None]


def solution(mesh):
    placed = (P("tm", None, None, "cells"), P("tm", "cells", None), P("tm", None), P("tm"))
    return jax.shard_map(
        on_device, mesh=mesh, in_specs=placed, out_specs=P("tm", "cells", None), check_vma=False
    )
```

time: 253 us -> 204 us (0.81); the launches traced: 252 us -> 200 us
  Pallas kernels: 247 us -> 195 us
    pallas_call x1, Pallas kernels: 247 us -> 195 us  [on_device(): pl.pallas_call(kernel, out_shape=jax.ShapeDtypeStruct((deep, wide), f32),...]
where the time goes in v2:
time: 204 us; the launch traced here: 200 us
  Pallas kernels  195 us (96%)
  local copies, waits for them, and re-layouts  3.81 us (2%)
    pallas_call x1, Pallas kernels, on_device(): pl.pallas_call(kernel, out_shape=jax.ShapeDtypeStruct((deep, wide), f32),...  195 us

profile of v2, /device:TPU:6, one launch (start us, length us, event | category | flops | bytes accessed | tf_op | source)
XLA Modules:
  0.0 200.1 jit_solution(13069366914617499953)
XLA Ops:
  0.7 0.8 compare_select_fusion
  1.4 0.7 broadcast_in_dim.14.scale
  2.1 194.9 %shard_map.46 = f32[256,2048]{1,0:T(8,128)} custom-call(f32[4,768,256]{2,1,0:T(8,128)} %bitcast.8, f32[256,2048]{1,0:T(8,128)} %bitcast.9, f32[24,128]{1,0:T(8,128)} %broadcast_in_dim.14.scale), custom_call_target="tpu_custom_call" | custom-call | tf_op jit(solution)/shard_map/pallas_call | solution.py:421
  197.0 3.1 %copy.7 = f32[1,256,2048]{2,1,0:T(8,128)} copy(f32[1,256,2048]{2,1,0:T(8,128)} %bitcast.7) | data formatting | bytes 4194304

commit v3 on v2

--- a/solution.py
+++ b/solution.py
@@ -10,10 +10,10 @@
 MESH = pl.DeviceIdType.MESH
 CHUNKS = 8
 LEAD = 2
-ORDER = [("late_sends", -3), ("late_relay", -2), ("forward", 0), ("turn", 0), ("adjoint", 4), ("sum_3", 2), ("sum_2", 1), ("relay_2", -1), ("back_2", 5), ("sum_1", 0), ("gather_2", 3), ("finish", 7), ("gather_1", 2), ("back_1", 4), ("cross_1", 5)]
+ORDER = [("late_sends", -3), ("late_relay", -2), ("forward", 0), ("turn", 0), ("gather_1", 3), ("adjoint", 4), ("sum_3", 2), ("sum_2", 1), ("relay_2", -1), ("back_2", 6), ("sum_1", 0), ("gather_2", 3), ("finish", 8), ("back_1", 5), ("cross_1", 6)]
 LAGS = 4
 
-S1, S3, Y3, R2, X2, Z1, Z3, P0, P2, P4, SA, SB, TB, GB, HB, GA, D2, D1, D3, E1, E2, E3, F1, V3, W3, SC = range(26)
+S1, S3, Y3, R2, X2, Z1, Z3, P0, P2, P4, SA, SB, TB, GB, HB, GA, D2, D1, D3, E1, E2, E3, F1, V3, W3, G2, G3, V1, W1, U1, SC = range(31)
 H1, H2, H3 = S1, R2, S3
 
 
@@ -56,7 +56,8 @@
         pl.semaphore_signal(barrier, inc=1, device_id=(lax.rem(t + by, tsize), other_y), device_id_type=MESH)
     for who in [other_core, other_y] + [z_peer(s) for s in range(1, nz)]:
         pl.semaphore_signal(barrier, inc=1, device_id=(t, who), device_id_type=MESH)
-    pl.semaphore_wait(barrier, 5 + 3 + 2 + gz)
+    with jax.named_scope('p_barrier'):
+        pl.semaphore_wait(barrier, 5 + 3 + 2 + gz)
 
     def copy(src, dst, kind, c, to_t, to_place, into=None):
         into = kind if into is None else into
@@ -78,14 +79,15 @@
         return pl.ds(pl.multiple_of(start, 8), size)
 
     first = core == 0
+    y_first = core == 0
     top = core * half
     pair = 2 * piece
-    mine = jnp.where(first, top + y * quarter + z * piece, top + z * pair + y * piece)
-    over_y = jnp.where(first, mine, top + z * pair + (1 - y) * piece)
+    mine = jnp.where(y_first, top + y * quarter + z * piece, top + z * pair + y * piece)
+    over_y = jnp.where(y_first, mine, top + z * pair + (1 - y) * piece)
     mine_y = top + y * quarter
     theirs_y = top + (1 - y) * quarter
     mine_z = top + z * pair
-    sides = ((first, piece, mine_y), (~first, pair, top))
+    sides = ((y_first, piece, mine_y), (~y_first, pair, top))
 
     relays_1 = (x == 1) | (x == 2)
     relays_3 = (t == 5) | (t == 6) | ((x == 3) & ~first)
@@ -102,17 +104,22 @@
         Z1: (t == 7, lambda c: copy(in3.at[c], hal.at[0, c], Z1, c, down(tsize - 3), place, S1)),
         Z3: (t == 7, lambda c: copy(in3.at[c], hal.at[2, c], Z3, c, down(tsize - 1), place, S3)),
         SA: (None, lambda c: copy(part.at[c, row((1 - core) * half, half)], got_a.at[c], SA, c, t, other_core)),
-        SB: (first, lambda c: copy(part.at[c, row(theirs_y, quarter)], got_b.at[c], SB, c, t, other_y)),
-        TB: (~first, lambda c: copy(part.at[c, row(over_y, piece)], got_b.at[c, 0:piece], TB, c, t, other_y, SB)),
-        GB: (first, lambda c: copy(full.at[c, row(mine_y, quarter)], full.at[c, row(mine_y, quarter)], GB, c, t, other_y)),
-        HB: (~first, lambda c: copy(full.at[c, row(mine, piece)], full.at[c, row(mine, piece)], HB, c, t, other_y, GB)),
+        SB: (y_first, lambda c: copy(part.at[c, row(theirs_y, quarter)], got_b.at[c], SB, c, t, other_y)),
+        TB: (~y_first, lambda c: copy(part.at[c, row(over_y, piece)], got_b.at[c, 0:piece], TB, c, t, other_y, SB)),
+        GB: (y_first, lambda c: copy(full.at[c, row(mine_y, quarter)], full.at[c, row(mine_y, quarter)], GB, c, t, other_y)),
+        HB: (~y_first, lambda c: copy(full.at[c, row(mine, piece)], full.at[c, row(mine, piece)], HB, c, t, other_y, GB)),
         GA: (None, lambda c: copy(full.at[c, row(core * half, half)], full.at[c, row(core * half, half)], GA, c, t, other_core)),
-        D2: (x >= 2, lambda c: copy(adj.at[1, c], in2.at[c], D2, c, down(tsize - 1), place)),
+        D2: ((x >= 2) & first, lambda c: copy(adj.at[1, c], in2.at[c], D2, c, down(tsize - 1), place)),
         D1: (x >= 1, lambda c: copy(adj.at[0, c], in1.at[c], D1, c, down(tsize - 1), place)),
         D3: (x == 3, lambda c: copy(adj.at[2, c], in3.at[c], D3, c, down(tsize - 3), place)),
         F1: (t == 7, lambda c: copy(in_a.at[c], in3.at[c], F1, c, down(tsize - 4), place, D3)),
-        V3: ((t == 4) | (t == 5), lambda c: copy(adj.at[2, c], in_a.at[c], V3, c, down(tsize - 4), other_y)),
-        W3: (t <= 1, lambda c: copy(in_a.at[c], in3.at[c], W3, c, down(1), other_y, D3)),
+        V3: (((t == 4) & first) | (t == 5), lambda c: copy(adj.at[2, c], in_a.at[c], V3, c, down(tsize - 4), other_y)),
+        G2: ((x == 2) & ~first, lambda c: copy(adj.at[1, c], in2.at[c], G2, c, down(1), place, D2)),
+        G3: ((x == 3) & ~first, lambda c: copy(adj.at[1, c], in_b.at[c], G3, c, down(tsize - 3), place, E2)),
+        V1: ((t == 4) & ~first, lambda c: copy(adj.at[2, c], in_a.at[c], V1, c, down(tsize - 4), place, V3)),
+        W1: ((t == 0) & ~first, lambda c: copy(in_a.at[c], in3.at[c], W1, c, down(1), place, D3)),
+        U1: ((t == 4) & ~first, lambda c: copy(in_b.at[c], in3.at[c], U1, c, down(1), place, D3)),
+        W3: (((t == 0) & first) | (t == 1), lambda c: copy(in_a.at[c], in3.at[c], W3, c, down(1), other_y, D3)),
         E1: ((t == 5) | (t == 6), lambda c: copy(adj.at[t - 4, c], in_a.at[c], E1, c, down(1), place)),
         E2: (t == 4, lambda c: copy(adj.at[1, c], in_b.at[c], E2, c, down(1), place)),
         E3: (t == 4, lambda c: copy(adj.at[0, c], in_b.at[c], E3, c, down(3), place, E2)),
@@ -220,30 +227,30 @@
         at = row(top, half)
         part[c, at, :] = part[c, at, :] + got_a[c]
         start(SB, c)
-        pl.when(~first)(lambda: spread(c, pair, top))
+        pl.when(~y_first)(lambda: spread(c, pair, top))
 
     def sum_2(c):
-        @pl.when(first)
+        @pl.when(y_first)
         def _():
             landed(got_b.at[c], SB, c)
             at = row(mine_y, quarter)
             part[c, at, :] = part[c, at, :] + got_b[c]
             spread(c, piece, mine_y)
 
-        @pl.when(~first)
+        @pl.when(~y_first)
         def _():
             at, total = collect(c, pair, top)
             part[c, at, :] = total
             start(TB, c, True)
 
     def sum_3(c):
-        @pl.when(first)
+        @pl.when(y_first)
         def _():
             at, total = collect(c, piece, mine_y)
             full[c, at, :] = total * scale[:, 0:1]
             share(c, piece, mine_y)
 
-        @pl.when(~first)
+        @pl.when(~y_first)
         def _():
             landed(got_b.at[c, 0:piece], SB, c)
             at = row(mine, piece)
@@ -251,19 +258,19 @@
             start(HB, c, True)
 
     def gather_1(c):
-        @pl.when(first)
+        @pl.when(y_first)
         def _():
             shared(c, piece, mine_y)
             start(GB, c, True)
 
-        @pl.when(~first)
+        @pl.when(~y_first)
         def _():
             landed(full.at[c, row(over_y, piece)], GB, c)
             share(c, pair, top)
 
     def gather_2(c):
-        landed(full.at[c, row(theirs_y, quarter)], GB, c, first)
-        pl.when(~first)(lambda: shared(c, pair, top))
+        landed(full.at[c, row(theirs_y, quarter)], GB, c, y_first)
+        pl.when(~y_first)(lambda: shared(c, pair, top))
         start(GA, c)
 
     def adjoint(c):
@@ -282,13 +289,16 @@
         adj[2, c] = block(3)
         adj[1, c] = block(2)
         start(D2, c)
+        start(G2, c)
+        start(G3, c)
         start(E2, c)
         start(E1, c, t == 5)
-        start(D3, c)
-        start(V3, c, t == 4)
+        start(D3, c, (x == 3) & first)
+        start(V3, c, (t == 4) & first)
+        start(V1, c)
         adj[0, c] = block(1)
         start(E3, c)
-        start(D1, c, x == 3)
+        start(D1, c, (x == 3) | ((x >= 1) & ~first))
         out[:, cols(c)] = block(0)
 
     def back_1(c):
@@ -304,11 +314,29 @@
             adj[2, c] = adj[2, c] + in_b[c]
             start(V3, c, True)
 
-        @pl.when(relays_1)
+        @pl.when(relays_1 & first)
         def _():
             landed(in2.at[c], D2, c)
             adj[0, c] = adj[0, c] + in2[c]
             start(D1, c, True)
+
+        @pl.when((x == 3) & ~first)
+        def _():
+            landed(in2.at[c], D2, c)
+            adj[2, c] = adj[2, c] + in2[c]
+            start(D3, c, True)
+
+        @pl.when((t == 0) & ~first)
+        def _():
+            landed(in_a.at[c], V3, c)
+            landed(in_b.at[c], E2, c)
+            in_a[c] = in_a[c] + in_b[c]
+            start(W1, c, True)
+
+        @pl.when((t == 4) & ~first)
+        def _():
+            landed(in_b.at[c], E2, c)
+            start(U1, c, True)
 
     def back_2(c):
         @pl.when(t == 7)
@@ -319,7 +347,7 @@
             start(F1, c, True)
 
     def cross_1(c):
-        landed(in_a.at[c], V3, c, t <= 1)
+        landed(in_a.at[c], V3, c, cp[W3][0])
         start(W3, c)
 
     def finish(c):
@@ -328,7 +356,7 @@
             landed(in1.at[c], D1, c)
             out[:, cols(c)] = out[:, cols(c)] + in1[c]
 
-        @pl.when(t <= 4)
+        @pl.when((t <= 4) | ((t == 5) & ~first))
         def _():
             landed(in3.at[c], D3, c)
             out[:, cols(c)] = out[:, cols(c)] + in3[c]
@@ -346,11 +374,14 @@
 
     for c in range(LEAD):
         own_sends(c)
-    split_rows(0)
-    split_rows(1)
-    relay_1(0)
-    split_rows(2)
-    split_rows(3)
+    with jax.named_scope('p_split'):
+        split_rows(0)
+        split_rows(1)
+    with jax.named_scope('p_relay'):
+        relay_1(0)
+    with jax.named_scope('p_split'):
+        split_rows(2)
+        split_rows(3)
     for lag in range(1, LAGS):
 
         @pl.when(t < lag)

time: 204 us -> 196 us (0.961)
  Pallas kernels: 195 us -> 188 us
    pallas_call x1, Pallas kernels: 195 us -> 188 us  [on_device(): pl.pallas_call(kernel, out_shape=jax.ShapeDtypeStruct((deep, wide), f32),...]
where the time goes in v3:
time: 196 us; the launch traced here: 193 us
  Pallas kernels  188 us (96%)
  local copies, waits for them, and re-layouts  3.81 us (2%)
    pallas_call x1, Pallas kernels, on_device(): pl.pallas_call(kernel, out_shape=jax.ShapeDtypeStruct((deep, wide), f32),...  188 us

profile of v3, /device:TPU:6, one launch (start us, length us, event | category | flops | bytes accessed | tf_op | source)
XLA Modules:
  0.0 192.9 jit_solution(3020683672699679557)
XLA Ops:
  0.7 0.8 compare_select_fusion
  1.4 0.7 broadcast_in_dim.14.scale
  2.1 187.7 %shard_map.46 = f32[256,2048]{1,0:T(8,128)} custom-call(f32[4,768,256]{2,1,0:T(8,128)} %bitcast.8, f32[256,2048]{1,0:T(8,128)} %bitcast.9, f32[24,128]{1,0:T(8,128)} %broadcast_in_dim.14.scale), custom_call_target="tpu_custom_call" | custom-call | tf_op jit(solution)/shard_map/pallas_call | solution.py:452
  189.7 3.1 %copy.7 = f32[1,256,2048]{2,1,0:T(8,128)} copy(f32[1,256,2048]{2,1,0:T(8,128)} %bitcast.7) | data formatting | bytes 4194304

commit v4 on v3

--- a/solution.py
+++ b/solution.py
@@ -10,7 +10,7 @@
 MESH = pl.DeviceIdType.MESH
 CHUNKS = 8
 LEAD = 2
-ORDER = [("late_sends", -3), ("late_relay", -2), ("forward", 0), ("turn", 0), ("gather_1", 3), ("adjoint", 4), ("sum_3", 2), ("sum_2", 1), ("relay_2", -1), ("back_2", 6), ("sum_1", 0), ("gather_2", 3), ("finish", 8), ("back_1", 5), ("cross_1", 6)]
+ORDER = [("late_sends", -2), ("late_relay", -2), ("forward", 0), ("turn", 0), ("gather_1", 3), ("adjoint", 4), ("sum_3", 2), ("sum_2", 1), ("relay_2", -1), ("back_2", 6), ("sum_1", 0), ("gather_2", 3), ("finish", 8), ("back_1", 5), ("cross_1", 6)]
 LAGS = 4
 
 S1, S3, Y3, R2, X2, Z1, Z3, P0, P2, P4, SA, SB, TB, GB, HB, GA, D2, D1, D3, E1, E2, E3, F1, V3, W3, G2, G3, V1, W1, U1, SC = range(31)

time: 196 us -> 206 us (1.051)
  Pallas kernels: 188 us -> 199 us
    pallas_call x1, Pallas kernels: 188 us -> 199 us  [on_device(): pl.pallas_call(kernel, out_shape=jax.ShapeDtypeStruct((deep, wide), f32),...]
where the time goes in v4:
time: 206 us; the launch traced here: 205 us
  Pallas kernels  199 us (97%)
  local copies, waits for them, and re-layouts  3.81 us (2%)
    pallas_call x1, Pallas kernels, on_device(): pl.pallas_call(kernel, out_shape=jax.ShapeDtypeStruct((deep, wide), f32),...  199 us

profile of v4, /device:TPU:6, one launch (start us, length us, event | category | flops | bytes accessed | tf_op | source)
XLA Modules:
  0.0 204.7 jit_solution(17790919301217717176)
XLA Ops:
  0.7 0.8 compare_select_fusion
  1.4 0.7 broadcast_in_dim.14.scale
  2.1 199.5 %shard_map.46 = f32[256,2048]{1,0:T(8,128)} custom-call(f32[4,768,256]{2,1,0:T(8,128)} %bitcast.8, f32[256,2048]{1,0:T(8,128)} %bitcast.9, f32[24,128]{1,0:T(8,128)} %broadcast_in_dim.14.scale), custom_call_target="tpu_custom_call" | custom-call | tf_op jit(solution)/shard_map/pallas_call | solution.py:452
  201.6 3.1 %copy.7 = f32[1,256,2048]{2,1,0:T(8,128)} copy(f32[1,256,2048]{2,1,0:T(8,128)} %bitcast.7) | data formatting | bytes 4194304
